TPU v7x, 512 devices: a whole 4x8x8 slice. The times are simulated.
512 devices in a mesh: stack: 128 (over z, y, core), azimuth: 2 (over x_hi), range: 2 (over x_lo).
Axes of the slice: x: 4 (x_hi: 2, x_lo: 2; x = x_hi * 2 + x_lo), y: 8, z: 8, core: 2. Of those that a mesh axis runs over, the one named last changes fastest.
Arguments:
- phases: bfloat16 [1152, 4, 32768], P('stack', 'azimuth', 'range'), may hold values from -6 to 6
- ifg_pairs: int32 [1152, 2], replicated, may hold values from 0 to 599, as said below
- preconditioner: float32 [600, 600], replicated, as said below
- coherence: int32 [4, 32768], P('azimuth', ('range', 'stack')), may hold values 0 or 1
- geo_tiles: int32 [4, 32768], P('azimuth', ('range', 'stack')), may hold values from 0 to 255, as said below
Outputs:
- deramped: float32 [600, 4, 32768], P(None, 'azimuth', ('range', 'stack'))
Inputs may be any that keep to these rules, and one draw needn't show every extreme that they name: `ifg_pairs`: each row names an earlier date first and a later date second. `preconditioner`: a symmetric matrix. geo_tiles[r, c] = min(max(floor((c + shift_r) / 128), 0), 255) with one integer shift_r per slab row, -32 <= shift_r <= 32; some row has shift -32 and another +32.
All inputs are finite; a program needn't handle non-finite values. No bound on the sum of `coherence` on one device may be relied on, other than what follows from the above.
Results may differ from a plain program's by a relative error of at most 0.002.
Values may be sent and summed in bfloat16 or wider, within the bound.
A program may use at most 64 MiB of HBM per device.

v0:
```python
import jax
import jax.numpy as jnp
from jax import lax
from jax.sharding import PartitionSpec as P

REWEIGHTS = 2
SKEW = 32


def from_behind(value, axis, steps):
    count = lax.axis_size(axis)
    pairs = [(source, (source + steps) % count) for source in range(count)]
    return lax.ppermute(value, axis, pairs)


def shifted_2(block, axis, distance):
    devices = range(lax.axis_size(axis))
    route = [(i - distance, i) for i in devices if i - distance in devices]
    return lax.ppermute(block, axis, route)


def plane_solve(gram_matrix, right_side):

    def entry(row_pos, col_pos):
        return gram_matrix[row_pos % 3, col_pos % 3]

    cofactors = [
        [
            entry(row_pos + 1, col_pos + 1) * entry(row_pos + 2, col_pos + 2)
            - entry(row_pos + 1, col_pos + 2) * entry(row_pos + 2, col_pos + 1)
            for col_pos in range(3)
        ]
        for row_pos in range(3)
    ]
    determinant = (
        entry(0, 0) * cofactors[0][0]
        + entry(0, 1) * cofactors[0][1]
        + entry(0, 2) * cofactors[0][2]
    )
    solution = [
        (
            cofactors[0][col_pos] * right_side[0]
            + cofactors[1][col_pos] * right_side[1]
            + cofactors[2][col_pos] * right_side[2]
        )
        / determinant
        for col_pos in range(3)
    ]
    return jnp.stack(solution)


def invert_pixels(stack_data, coherence_row, incidence, incidence_half, preconditioner):
    normal_rhs = lax.dot_general(
        incidence_half, stack_data, (((0,), (0,)), ((), ())), preferred_element_type=jnp.float32
    )
    series = jnp.dot(
        preconditioner,
        normal_rhs,
        precision=lax.Precision.HIGHEST,
        preferred_element_type=jnp.float32,
    )
    values = stack_data.astype(jnp.float32)
    for sweep in range(REWEIGHTS):
        predicted = jnp.dot(
            incidence, series, precision=lax.Precision.HIGHEST, preferred_element_type=jnp.float32
        )
        residual = values - predicted
        square = residual * residual
        robust_scale = jnp.mean(square, axis=0) + 1e-06
        shifted = square + robust_scale
        weight = coherence_row * (robust_scale * robust_scale) / (shifted * shifted)
        update = lax.dot_general(
            incidence,
            weight * residual,
            (((0,), (0,)), ((), ())),
            precision=lax.Precision.HIGHEST,
            preferred_element_type=jnp.float32,
        )
        series = series + jnp.dot(
            preconditioner,
            update,
            precision=lax.Precision.HIGHEST,
            preferred_element_type=jnp.float32,
        )
    return series


def tile_moments(series_part, weight, coord_u, coord_v):
    date_total = series_part.shape[0]
    basis = jnp.stack([jnp.ones_like(coord_u), coord_u, coord_v]).reshape(3, -1)
    weighted_basis = basis * weight.reshape(1, -1)
    moments = lax.dot_general(
        weighted_basis,
        series_part.reshape(date_total, -1),
        (((1,), (1,)), ((), ())),
        precision=lax.Precision.HIGHEST,
        preferred_element_type=jnp.float32,
    )
    gram_matrix = lax.dot_general(
        weighted_basis,
        basis,
        (((1,), (1,)), ((), ())),
        precision=lax.Precision.HIGHEST,
        preferred_element_type=jnp.float32,
    )
    return (moments, gram_matrix)


def plane_at(plane_coefs, coord_u, coord_v):
    return (
        plane_coefs[0][:, None, None]
        + plane_coefs[1][:, None, None] * coord_u[None]
        + plane_coefs[2][:, None, None] * coord_v[None]
    )


def pixel_from_lower(values, stack_pos):
    wrapped = from_behind(values, "stack", 1)
    across = shifted_2(wrapped.astype(jnp.bfloat16), "range", 1).astype(wrapped.dtype)
    return jnp.where(stack_pos == 0, across, wrapped)


def pixel_from_upper(values, stack_pos, last_pos):
    wrapped = from_behind(values, "stack", -1)
    across = shifted_2(wrapped.astype(jnp.bfloat16), "range", -1).astype(wrapped.dtype)
    return jnp.where(stack_pos == last_pos, across, wrapped)


def local(phases, ifg_pairs, preconditioner, coherence, geo_tiles):
    stacked = lax.all_to_all(phases, "stack", split_axis=2, concat_axis=0, tiled=True)
    ifg_total, row_local, col_local = stacked.shape
    pixel_count = row_local * col_local
    stack_data = stacked.reshape(ifg_total, pixel_count)
    date_total = preconditioner.shape[0]
    stack_size = lax.axis_size("stack")
    range_size = lax.axis_size("range")
    azimuth_size = lax.axis_size("azimuth")
    edge = SKEW
    earlier_date = ifg_pairs[:, 0]
    later_date = ifg_pairs[:, 1]
    date_ids = jnp.arange(date_total, dtype=jnp.int32)
    incidence = (later_date[:, None] == date_ids).astype(jnp.float32) - (
        earlier_date[:, None] == date_ids
    ).astype(jnp.float32)
    incidence_half = incidence.astype(jnp.bfloat16)
    coherence_f = coherence.astype(jnp.float32)
    series = invert_pixels(
        stack_data, coherence_f.reshape(-1), incidence, incidence_half, preconditioner
    )
    series3 = series.reshape(date_total, row_local, col_local)
    stack_pos = lax.axis_index("stack")
    last_pos = stack_size - 1
    block_index = lax.axis_index("range") * stack_size + stack_pos
    row_ids = lax.axis_index("azimuth") * row_local + jnp.arange(row_local, dtype=jnp.int32)
    row_coord = (row_ids.astype(jnp.float32) + 0.5) / (row_local * azimuth_size) - 0.5

    def coords(first_col, width):
        col_ids = first_col + jnp.arange(width, dtype=jnp.int32)
        col_coord = (col_ids.astype(jnp.float32) + 0.5) / (
            col_local * stack_size * range_size
        ) - 0.5
        return (
            jnp.broadcast_to(row_coord[:, None], (row_local, width)),
            jnp.broadcast_to(col_coord[None, :], (row_local, width)),
        )

    own_u, own_v = coords(block_index * col_local, col_local)
    lower_member = (geo_tiles == block_index - 1).astype(jnp.float32)
    upper_member = (geo_tiles == block_index + 1).astype(jnp.float32)
    own_weight = coherence_f * (geo_tiles == block_index).astype(jnp.float32)
    own_moments, own_gram = tile_moments(series3, own_weight, own_u, own_v)
    identity = jnp.eye(3, dtype=jnp.float32)
    left_member = lower_member[:, :edge]
    right_member = upper_member[:, col_local - edge :]
    left_send = jnp.concatenate(
        [series3[:, :, :edge], (coherence_f[:, :edge] * left_member)[None]], axis=0
    )
    right_send = jnp.concatenate(
        [
            series3[:, :, col_local - edge :],
            (coherence_f[:, col_local - edge :] * right_member)[None],
        ],
        axis=0,
    )
    from_upper = pixel_from_upper(left_send, stack_pos, last_pos)
    from_lower = pixel_from_lower(right_send, stack_pos)
    upper_u, upper_v = coords((block_index + 1) * col_local, edge)
    lower_u, lower_v = coords(block_index * col_local - edge, edge)
    upper_moments, upper_gram = tile_moments(
        from_upper[:date_total], from_upper[date_total], upper_u, upper_v
    )
    lower_moments, lower_gram = tile_moments(
        from_lower[:date_total], from_lower[date_total], lower_u, lower_v
    )
    moments = own_moments + upper_moments + lower_moments
    gram_matrix = own_gram + upper_gram + lower_gram
    moments, gram_matrix = lax.psum((moments, gram_matrix), "azimuth")
    plane_coefs = plane_solve(gram_matrix + identity, moments)
    own_flat = series3 - plane_at(plane_coefs, own_u, own_v)
    upper_flat = from_upper[:date_total] - plane_at(plane_coefs, upper_u, upper_v)
    lower_flat = from_lower[:date_total] - plane_at(plane_coefs, lower_u, lower_v)
    back_right = pixel_from_upper(lower_flat, stack_pos, last_pos)
    back_left = pixel_from_lower(upper_flat, stack_pos)
    left_final = jnp.where(left_member[None] > 0.5, back_left, own_flat[:, :, :edge])
    right_final = jnp.where(
        right_member[None] > 0.5, back_right, own_flat[:, :, col_local - edge :]
    )
    result = jnp.concatenate(
        [left_final, own_flat[:, :, edge : col_local - edge], right_final], axis=2
    )
    return result


def solution(mesh):
    return jax.shard_map(
        local,
        mesh=mesh,
        in_specs=(
            P("stack", "azimuth", "range"),
            P(),
            P(),
            P("azimuth", ("range", "stack")),
            P("azimuth", ("range", "stack")),
        ),
        out_specs=P(None, "azimuth", ("range", "stack")),
        check_vma=False,
    )
```

profile of v0, /device:TPU:4, one launch (start us, length us, event | category | flops | bytes accessed | tf_op | source)
XLA Modules:
  0.0 209.7 jit_solution(1369464189957789960)
XLA Ops:
  0.0 15.9 %copy.28 = bf16[9,2,16384]{0,1,2:T(2,128)(2,1)} copy(bf16[9,2,16384]{2,1,0:T(2,128)(2,1)} %param.5) | data formatting | bytes 1179648 | tf_op args[0]
  15.9 18.3 %reshape.182 = bf16[128,2,1152]{2,1,0:T(2,128)(2,1)} reshape(bf16[16384,2,9]{2,1,0:T(2,128)(2,1)} %bitcast.65) | data formatting | bytes 1179648
  34.2 17.8 %all-to-all-start = ((bf16[128,2,1152]{2,1,0:T(2,128)(2,1)}), bf16[128,2,1152]{2,1,0:T(2,128)(2,1)S(1)}, u32[]{:S(2)}, u32[]{:S(2)}) async-start(bf16[128,2,1152]{2,1,0:T(2,128)(2,1)} %reshape.182), calls=%async_computation | async-start | bytes 1179648 | tf_op jit(solution)/shard_map/all_to_all | solution.py:130
  52.1 0.1 copy.31
  52.3 20.2 %all-to-all-done = bf16[128,2,1152]{2,1,0:T(2,128)(2,1)S(1)} async-done(((bf16[128,2,1152]{2,1,0:T(2,128)(2,1)}), bf16[128,2,1152]{2,1,0:T(2,128)(2,1)S(1)}, u32[]{:S(2)}, u32[]{:S(2)}) %all-to-all-start) | async-done | bytes 589856 | tf_op jit(solution)/shard_map/all_to_all | solution.py:130
  72.5 19.2 %reshape.183 = bf16[16384,2,9]{2,1,0:T(2,128)(2,1)} reshape(bf16[128,2,1152]{2,1,0:T(2,128)(2,1)S(1)} %all-to-all-done) | data formatting | bytes 1179648
  91.8 16.7 %copy.29 = bf16[9,2,128,128]{3,1,0,2:T(2,128)(2,1)S(1)} copy(bf16[9,2,128,128]{0,1,3,2:T(2,128)(2,1)} %bitcast.64) | data formatting | bytes 1179648 | tf_op jit(solution)/shard_map/all_to_all | solution.py:130
  108.5 1.2 fusion.7
  109.7 1.6 fusion.77
  111.3 3.6 %multiply_reduce_fusion.1 = (f32[256]{0:T(256)S(1)}, f32[1152,256]{1,0:T(8,128)S(1)}) fusion(f32[256,600]{0,1:T(8,128)S(1)} %fusion.77, s32[1152]{0:T(1024)S(1)} %get-tuple-element.9, s32[1152]{0:T(1024)S(1)} %get-tuple-element.8, bf16[144,8,2,128]{3,2,1,0:T(2,128)(2,1)S(1)} %bitcast.70), kind=kOutput, calls=%fused_computation.34 | convolution fusion | flops 2128001792 | bytes 2394112 | tf_op jit(solution)/shard_map/dot_general | solution.py:64
  115.0 5.4 %fusion.2 = f32[600,256]{1,0:T(8,128)S(1)} fusion(s32[1152]{0:T(1024)S(1)} %get-tuple-element.9, s32[1152]{0:T(1024)S(1)} %get-tuple-element.8, f32[1152,256]{1,0:T(8,128)S(1)} %get-tuple-element.36, f32[256]{0:T(256)S(1)} %get-tuple-element.34, f32[256]{0:T(256)S(1)} %get-tuple-element.33), kind=kOutput, calls=%fused_computation.4 | convolution fusion | flops 2128296960 | bytes 1805312 | tf_op jit(solution)/shard_map/dot_general | solution.py:72
  120.3 1.9 convolution_add_fusion.1
  122.2 3.7 %multiply_reduce_fusion = (f32[256]{0:T(256)S(1)}, f32[1152,256]{1,0:T(8,128)S(1)}) fusion(f32[256,600]{0,1:T(8,128)S(1)} %convolution_add_fusion.1, s32[1152]{0:T(1024)S(1)} %get-tuple-element.9, s32[1152]{0:T(1024)S(1)} %get-tuple-element.8, bf16[144,8,2,128]{3,2,1,0:T(2,128)(2,1)S(1)} %bitcast.71), kind=kOutput, calls=%fused_computation.32 | convolution fusion | flops 2128001792 | bytes 2394112 | tf_op jit(solution)/shard_map/dot_general | solution.py:64
  125.9 5.4 %fusion = f32[600,256]{1,0:T(8,128)S(1)} fusion(s32[1152]{0:T(1024)S(1)} %get-tuple-element.9, s32[1152]{0:T(1024)S(1)} %get-tuple-element.8, f32[1152,256]{1,0:T(8,128)S(1)} %get-tuple-element.38, f32[256]{0:T(256)S(1)} %get-tuple-element.32, f32[256]{0:T(256)S(1)} %get-tuple-element.31), kind=kOutput, calls=%fused_computation.2 | convolution fusion | flops 2128296960 | bytes 1805312 | tf_op jit(solution)/shard_map/dot_general | solution.py:72
  131.3 1.7 convolution_add_fusion
  133.0 0.5 copy.36
  133.5 0.1 pad_maximum_fusion.1
  133.6 3.2 %collective-permute-start = (f32[601,2,32]{0,2,1:T(8,128)S(1)}, f32[601,2,32]{0,2,1:T(8,128)S(1)}, u32[]{:S(2)}, u32[]{:S(2)}) collective-permute-start(f32[601,2,32]{0,2,1:T(8,128)S(1)} %pad_maximum_fusion.1), channel_id=1, source_target_pairs={{0,508},{4,0},{8,4},{12,8},{16,12},{20,16},{24,20},{28,24},{32,28}... | collective-permute-start | bytes 461576 | tf_op jit(solution)/shard_map/ppermute | solution.py:13
  136.8 0.1 copy.33
  136.9 0.1 pad_maximum_fusion.2
  137.0 1.9 collective-permute-start.2
  138.9 0.7 collective-permute-done
  139.6 1.3 collective-permute-start.1
  141.0 0.6 fusion.48
  141.6 5.4 %collective-permute-done.2 = f32[601,2,32]{0,2,1:T(8,128)S(1)} collective-permute-done((f32[601,2,32]{0,2,1:T(8,128)S(1)}, f32[601,2,32]{0,2,1:T(8,128)S(1)}, u32[]{:S(2)}, u32[]{:S(2)}) %collective-permute-start.2) | collective-permute-done | bytes 153888 | tf_op jit(solution)/shard_map/ppermute | solution.py:13
  147.0 3.1 %collective-permute-start.3 = (bf16[601,2,32]{0,2,1:T(8,128)(2,1)S(1)}, bf16[601,2,32]{0,2,1:T(8,128)(2,1)S(1)}, u32[]{:S(2)}, u32[]{:S(2)}) collective-permute-start(bf16[601,2,32]{0,2,1:T(8,128)(2,1)S(1)} %convert_element_type.68), channel_id=1, source_target_pairs={{0,1},{2,3},{4,5},{6,7},{8,9},{10,11},{12,13},{14,15},{16,17},{18,... | collective-permute-start | bytes 230792 | tf_op jit(solution)/shard_map/ppermute | solution.py:19
  150.1 0.2 slice_reduce_fusion.1
  150.4 0.3 fusion.30
  150.7 0.2 convolution_bitcast_fusion.3
  150.9 1.2 collective-permute-done.3
  152.1 0.2 slice_reduce_fusion
  152.3 0.2 convolution_bitcast_fusion.2
  152.5 0.3 fusion.29
  152.9 0.2 fusion.32
  153.1 8.9 %all-reduce = (f32[3,3]{1,0:T(4,128)S(1)}, f32[3,600]{1,0:T(4,128)S(1)}) all-reduce(f32[3,3]{1,0:T(4,128)S(1)} %fusion.32, f32[3,600]{1,0:T(4,128)S(1)} %fusion.29), channel_id=1, replica_groups=mesh['stack'=128,'azimuth'=2,'range'=2] {'azimuth'}, use_global_device_ids=true, to_apply=%region_2.3 | all-reduce | flops 1809 | bytes 14472 | tf_op jit(solution)/shard_map/psum | solution.py:197
  162.0 0.7 fusion.76
  187.2 0.1 add_subtract_fusion.2
  187.3 1.9 collective-permute-start.4
  189.2 7.0 %collective-permute-start.6 = (f32[600,2,32]{0,2,1:T(8,128)S(1)}, f32[600,2,32]{0,2,1:T(8,128)S(1)}, u32[]{:S(2)}, u32[]{:S(2)}) collective-permute-start(f32[600,2,32]{0,2,1:T(8,128)S(1)} %get-tuple-element.17), channel_id=1, source_target_pairs={{0,508},{4,0},{8,4},{12,8},{16,12},{20,16},{24,20},{28,24},{32,28}... | collective-permute-start | bytes 460808 | tf_op jit(solution)/shard_map/ppermute | solution.py:13
  196.2 0.1 fusion.65
  196.2 1.0 collective-permute-done.4
  197.2 4.9 %collective-permute-start.5 = (bf16[600,2,32]{0,2,1:T(8,128)(2,1)S(1)}, bf16[600,2,32]{0,2,1:T(8,128)(2,1)S(1)}, u32[]{:S(2)}, u32[]{:S(2)}) collective-permute-start(bf16[600,2,32]{0,2,1:T(8,128)(2,1)S(1)} %convert_element_type.71), channel_id=1, source_target_pairs={{0,1},{2,3},{4,5},{6,7},{8,9},{10,11},{12,13},{14,15},{16,17},{18,... | collective-permute-start | bytes 230408 | tf_op jit(solution)/shard_map/ppermute | solution.py:19
  202.2 1.3 collective-permute-start.7
  203.5 0.1 add_subtract_fusion
  203.6 0.5 collective-permute-done.5
  204.2 4.3 %collective-permute-done.7 = bf16[600,2,32]{0,2,1:T(8,128)(2,1)S(1)} collective-permute-done((bf16[600,2,32]{0,2,1:T(8,128)(2,1)S(1)}, bf16[600,2,32]{0,2,1:T(8,128)(2,1)S(1)}, u32[]{:S(2)}, u32[]{:S(2)}) %collective-permute-start.7) | collective-permute-done | bytes 76832 | tf_op jit(solution)/shard_map/ppermute | solution.py:19
  208.5 0.1 slice_select_fusion.1
  208.7 1.1 copy.35
  (37 shorter events, 0.6 us)
Async XLA Ops:
  0.0 109.7 %copy-start = (f32[600,600]{1,0:T(8,128)S(1)}, f32[600,600]{1,0:T(8,128)}, u32[]{:S(2)}) copy-start(f32[600,600]{1,0:T(8,128)} %param.7) | copy-start | bytes 4320004
  15.9 36.1 %copy-start.1 = (s32[2,128]{1,0:T(2,128)S(1)}, s32[2,128]{1,0:T(2,128)}, u32[]{:S(2)}) copy-start(s32[2,128]{1,0:T(2,128)} %param.8) | copy-start | bytes 3076
  15.9 36.1 %copy-start.3 = (s32[2,128]{1,0:T(2,128)S(1)}, s32[2,128]{1,0:T(2,128)}, u32[]{:S(2)}) copy-start(s32[2,128]{1,0:T(2,128)} %param.9) | copy-start | bytes 3076
  15.9 36.3 %copy-start.2 = (s32[1152,2]{0,1:T(2,128)S(1)}, s32[1152,2]{0,1:T(2,128)}, u32[]{:S(2)}) copy-start(s32[1152,2]{0,1:T(2,128)} %param.6) | copy-start | bytes 27652
  34.2 38.3 %all-to-all-start = ((bf16[128,2,1152]{2,1,0:T(2,128)(2,1)}), bf16[128,2,1152]{2,1,0:T(2,128)(2,1)S(1)}, u32[]{:S(2)}, u32[]{:S(2)}) async-start(bf16[128,2,1152]{2,1,0:T(2,128)(2,1)} %reshape.182), calls=%async_computation | async-start | bytes 1179648 | tf_op jit(solution)/shard_map/all_to_all | solution.py:130
  133.6 6.0 %collective-permute-start = (f32[601,2,32]{0,2,1:T(8,128)S(1)}, f32[601,2,32]{0,2,1:T(8,128)S(1)}, u32[]{:S(2)}, u32[]{:S(2)}) collective-permute-start(f32[601,2,32]{0,2,1:T(8,128)S(1)} %pad_maximum_fusion.1), channel_id=1, source_target_pairs={{0,508},{4,0},{8,4},{12,8},{16,12},{20,16},{24,20},{28,24},{32,28}... | collective-permute-start | bytes 461576 | tf_op jit(solution)/shard_map/ppermute | solution.py:13
  137.0 9.9 %collective-permute-start.2 = (f32[601,2,32]{0,2,1:T(8,128)S(1)}, f32[601,2,32]{0,2,1:T(8,128)S(1)}, u32[]{:S(2)}, u32[]{:S(2)}) collective-permute-start(f32[601,2,32]{0,2,1:T(8,128)S(1)} %pad_maximum_fusion.2), channel_id=1, source_target_pairs={{0,4},{4,8},{8,12},{12,16},{16,20},{20,24},{24,28},{28,32},{32,36}... | collective-permute-start | bytes 461576 | tf_op jit(solution)/shard_map/ppermute | solution.py:13
  139.6 10.4 %collective-permute-start.1 = (bf16[601,2,32]{0,2,1:T(8,128)(2,1)S(1)}, bf16[601,2,32]{0,2,1:T(8,128)(2,1)S(1)}, u32[]{:S(2)}, u32[]{:S(2)}) collective-permute-start(bf16[601,2,32]{0,2,1:T(8,128)(2,1)S(1)} %convert_element_type.62), channel_id=1, source_target_pairs={{1,0},{3,2},{5,4},{7,6},{9,8},{11,10},{13,12},{15,14},{17,16},{19,... | collective-permute-start | bytes 230792 | tf_op jit(solution)/shard_map/ppermute | solution.py:19
  147.0 5.1 %collective-permute-start.3 = (bf16[601,2,32]{0,2,1:T(8,128)(2,1)S(1)}, bf16[601,2,32]{0,2,1:T(8,128)(2,1)S(1)}, u32[]{:S(2)}, u32[]{:S(2)}) collective-permute-start(bf16[601,2,32]{0,2,1:T(8,128)(2,1)S(1)} %convert_element_type.68), channel_id=1, source_target_pairs={{0,1},{2,3},{4,5},{6,7},{8,9},{10,11},{12,13},{14,15},{16,17},{18,... | collective-permute-start | bytes 230792 | tf_op jit(solution)/shard_map/ppermute | solution.py:19
  187.3 10.0 %collective-permute-start.4 = (f32[600,2,32]{0,2,1:T(8,128)S(1)}, f32[600,2,32]{0,2,1:T(8,128)S(1)}, u32[]{:S(2)}, u32[]{:S(2)}) collective-permute-start(f32[600,2,32]{0,2,1:T(8,128)S(1)} %get-tuple-element.16), channel_id=1, source_target_pairs={{0,4},{4,8},{8,12},{12,16},{16,20},{20,24},{24,28},{28,32},{32,36}... | collective-permute-start | bytes 460808 | tf_op jit(solution)/shard_map/ppermute | solution.py:13
  189.2 13.0 %collective-permute-start.6 = (f32[600,2,32]{0,2,1:T(8,128)S(1)}, f32[600,2,32]{0,2,1:T(8,128)S(1)}, u32[]{:S(2)}, u32[]{:S(2)}) collective-permute-start(f32[600,2,32]{0,2,1:T(8,128)S(1)} %get-tuple-element.17), channel_id=1, source_target_pairs={{0,508},{4,0},{8,4},{12,8},{16,12},{20,16},{24,20},{28,24},{32,28}... | collective-permute-start | bytes 460808 | tf_op jit(solution)/shard_map/ppermute | solution.py:13
  197.2 6.9 %collective-permute-start.5 = (bf16[600,2,32]{0,2,1:T(8,128)(2,1)S(1)}, bf16[600,2,32]{0,2,1:T(8,128)(2,1)S(1)}, u32[]{:S(2)}, u32[]{:S(2)}) collective-permute-start(bf16[600,2,32]{0,2,1:T(8,128)(2,1)S(1)} %convert_element_type.71), channel_id=1, source_target_pairs={{0,1},{2,3},{4,5},{6,7},{8,9},{10,11},{12,13},{14,15},{16,17},{18,... | collective-permute-start | bytes 230408 | tf_op jit(solution)/shard_map/ppermute | solution.py:19
  202.2 6.3 %collective-permute-start.7 = (bf16[600,2,32]{0,2,1:T(8,128)(2,1)S(1)}, bf16[600,2,32]{0,2,1:T(8,128)(2,1)S(1)}, u32[]{:S(2)}, u32[]{:S(2)}) collective-permute-start(bf16[600,2,32]{0,2,1:T(8,128)(2,1)S(1)} %convert_element_type.73), channel_id=1, source_target_pairs={{1,0},{3,2},{5,4},{7,6},{9,8},{11,10},{13,12},{15,14},{17,16},{19,... | collective-permute-start | bytes 230408 | tf_op jit(solution)/shard_map/ppermute | solution.py:19
where the time goes:
time: 212 us; the launch traced here: 210 us
  local copies, waits for them, and re-layouts  73.1 us (34%)
  starting transfers between devices  42.4 us (20%)
  waiting for transfers between devices  33.4 us (16%)
  matrix products  26.2 us (12%)
  between operations  24.8 us (12%)
  blocking collectives  8.9 us (4%)
    unnamed x11, local copies, waits for them, and re-layouts  53.4 us
    all_to_all x1, waiting for transfers between devices, local(): lax.all_to_all(phases, 'stack', split_axis=2, concat_axis=0, tiled=True)  20.2 us
    all_to_all x1, starting transfers between devices, local(): lax.all_to_all(phases, 'stack', split_axis=2, concat_axis=0, tiled=True)  17.8 us
    all_to_all x1, local copies, waits for them, and re-layouts, local(): lax.all_to_all(phases, 'stack', split_axis=2, concat_axis=0, tiled=True)  16.7 us
    ppermute x4, starting transfers between devices, from_behind(): return lax.ppermute(value, axis, pairs)  14 us
    dot_general x2, matrix products, invert_pixels(): lax.dot_general(incidence, weight * residual, (((0,), (0,)), ((), ())), p...  10.7 us
    ppermute x4, starting transfers between devices, shifted_2(): return lax.ppermute(block, axis, route)  10.6 us
    psum x1, blocking collectives, local(): moments, gram_matrix = lax.psum((moments, gram_matrix), 'azimuth')  8.9 us
  transfers between devices with their start and end apart: 9, of which 7 were waited for; matrix products, arithmetic and copies ran while one was open for 1% of the time, Pallas kernels for 0%

commit v1 on v0

v1 whole, which is shorter than its diff:
```python
import functools

import jax
import jax.numpy as jnp
from jax import lax
from jax.experimental import pallas as pl
from jax.experimental.pallas import tpu as pltpu
from jax.sharding import PartitionSpec as P

MESH = pl.DeviceIdType.MESH
F32 = jnp.float32
BF16 = jnp.bfloat16
REWEIGHTS = 2
IFGS = 1152
DATES = 600
DATE_ROWS = 608
DATE_LANES = 640
COLS = 128
ROWS = 2
PIXELS = ROWS * COLS
SLAB_ROWS = 4
SLAB_COLS = 32768
STACK = 128
SIDE = 8
OWN_IFGS = IFGS // STACK
BLOCKS = SLAB_COLS // COLS
REACH = (-2, -1, 0, 1, 2)


def split(value):
    high = value.astype(BF16)
    return high, (value - high.astype(F32)).astype(BF16)


def dot(left, right):
    return jnp.dot(left, right, preferred_element_type=F32)


def ring_hops(step):
    return min(step % SIDE, -step % SIDE)


def far_first():
    steps = [(dz, dy, dc) for dz in range(SIDE) for dy in range(SIDE) for dc in range(2)]
    steps.remove((0, 0, 0))
    return sorted(steps, key=lambda step: -ring_hops(step[0]) - ring_hops(step[1]))


def invert_kernel(
    phases,
    pairs,
    precond,
    coherence,
    tiles,
    series_out,
    moments_out,
    solve_out,
    stacked,
    wide,
    values,
    values_half,
    pairs_v,
    precond_v,
    precond_pad,
    coherence_v,
    tiles_v,
    incidence,
    incidence_t,
    gain_hi,
    gain_lo,
    series,
    series_hi,
    series_lo,
    pull_hi,
    pull_lo,
    gram_own,
    gram_got,
    moments_own,
    moments_got,
    moments_all,
    solve_v,
    load_sem,
    store_sem,
    phase_send,
    phase_recv,
    gram_send,
    gram_recv,
    moment_send,
    moment_recv,
):
    me = lax.axis_index("stack")
    azimuth = lax.axis_index("azimuth")
    block = lax.axis_index("range") * STACK + me
    z, y, core = me // (2 * SIDE), lax.rem(me // 2, SIDE), lax.rem(me, 2)

    def peer(reach, other):
        there = lax.rem(block + reach + BLOCKS, BLOCKS)
        return {
            "stack": lax.rem(there, STACK),
            "azimuth": (1 - azimuth) if other else azimuth,
            "range": there // STACK,
        }

    group = [(reach, other) for other in (0, 1) for reach in REACH if reach or other]

    barrier = pltpu.get_barrier_semaphore()

    def greet(step, carry):
        pl.semaphore_signal(
            barrier, inc=1, device_id={"stack": lax.rem(me + step, STACK)}, device_id_type=MESH
        )
        return carry

    lax.fori_loop(1, STACK, greet, 0)
    for reach, other in group:
        pl.semaphore_signal(barrier, inc=1, device_id=peer(reach, other), device_id_type=MESH)

    small = [
        pltpu.make_async_copy(coherence, coherence_v, load_sem.at[0]),
        pltpu.make_async_copy(tiles, tiles_v, load_sem.at[1]),
        pltpu.make_async_copy(pairs, pairs_v, load_sem.at[2]),
        pltpu.make_async_copy(precond, precond_v, load_sem.at[3]),
        pltpu.make_async_copy(
            phases.at[:, :, pl.ds(pl.multiple_of(me * COLS, COLS), COLS)],
            stacked.at[pl.ds(OWN_IFGS * me, OWN_IFGS)],
            load_sem.at[4],
        ),
    ]
    for copy in small:
        copy.start()

    pl.semaphore_wait(barrier, STACK - 1 + len(group))

    for dz, dy, dc in far_first():
        there = (
            lax.rem(z + dz, SIDE) * (2 * SIDE) + lax.rem(y + dy, SIDE) * 2 + lax.rem(core + dc, 2)
        )
        pltpu.make_async_remote_copy(
            src_ref=phases.at[:, :, pl.ds(pl.multiple_of(there * COLS, COLS), COLS)],
            dst_ref=stacked.at[pl.ds(OWN_IFGS * me, OWN_IFGS)],
            send_sem=phase_send,
            recv_sem=phase_recv,
            device_id={"stack": there},
            device_id_type=MESH,
        ).start()

    small[0].wait()
    small[1].wait()
    coh = coherence_v[...].astype(F32)
    tile_ids = tiles_v[...]
    column = lax.broadcasted_iota(jnp.int32, (1, COLS), 1).astype(F32)
    row_u = [
        ((azimuth * ROWS + row).astype(F32) + 0.5) / SLAB_ROWS - 0.5 for row in range(ROWS)
    ]
    offset_v = [(column - (63.5 + COLS * tile)) / SLAB_COLS for tile in (-1, 0, 1)]
    members = [(tile_ids == block + tile).astype(F32) for tile in (-1, 0, 1)]
    weights = [coh * member for member in members]

    def lanes(pieces):
        return jnp.concatenate(pieces, axis=1)

    basis_rows = []
    for tile in range(3):
        ones = jnp.ones((1, COLS), F32)
        basis_rows.append(
            [
                lanes([ones, ones]),
                lanes([ones * row_u[0], ones * row_u[1]]),
                lanes([offset_v[tile], offset_v[tile]]),
            ]
        )
        w0, w1 = weights[tile][0:1], weights[tile][1:2]
        dv = offset_v[tile]
        both, lean = w0 + w1, w0 * row_u[0] + w1 * row_u[1]
        gram_own[tile] = jnp.concatenate(
            [
                both,
                lean,
                both * dv,
                w0 * (row_u[0] * row_u[0]) + w1 * (row_u[1] * row_u[1]),
                lean * dv,
                both * dv * dv,
                jnp.zeros((2, COLS), F32),
            ],
            axis=0,
        )

    def trade(own, got, send_sem, recv_sem):
        copies = []
        for reach, other in group:
            first, last = max(0, reach), min(3, 3 + reach)
            copies.append(
                pltpu.make_async_remote_copy(
                    src_ref=own.at[pl.ds(first, last - first)],
                    dst_ref=got.at[other, reach + 2, pl.ds(first - reach, last - first)],
                    send_sem=send_sem.at[other, reach + 2],
                    recv_sem=recv_sem.at[other, reach + 2],
                    device_id=peer(reach, other),
                    device_id_type=MESH,
                )
            )
        for copy in copies:
            copy.start()
        return copies

    def gathered(own, got):
        totals = []
        for tile in range(3):
            total = own[tile]
            for reach, other in group:
                if max(0, reach) - reach <= tile < min(3, 3 + reach) - reach:
                    total = total + got[other, reach + 2, tile]
            totals.append(total)
        return totals

    gram_copies = trade(gram_own, gram_got, gram_send, gram_recv)

    small[2].wait()
    earlier, later = pairs_v[0:1, :], pairs_v[1:2, :]
    date_rows = lax.broadcasted_iota(jnp.int32, (DATE_LANES, IFGS), 0)
    incidence_t[...] = (
        jnp.where(later == date_rows, 1.0, 0.0) - jnp.where(earlier == date_rows, 1.0, 0.0)
    ).astype(BF16)
    later_col = jnp.broadcast_to(later.astype(F32), (COLS, IFGS)).T
    earlier_col = jnp.broadcast_to(earlier.astype(F32), (COLS, IFGS)).T
    for part in range(DATE_LANES // 128):
        date_lanes = (
            lax.broadcasted_iota(jnp.int32, (IFGS, 128), 1) + 128 * part
        ).astype(F32)
        incidence[:, 128 * part : 128 * part + 128] = (
            jnp.where(later_col == date_lanes, 1.0, 0.0)
            - jnp.where(earlier_col == date_lanes, 1.0, 0.0)
        ).astype(BF16)
    precond_pad[...] = jnp.zeros((DATE_ROWS, DATE_LANES), F32)
    small[3].wait()
    precond_pad[0:DATES, 0:DATES] = precond_v[...]
    first_hi, first_lo = split(precond_pad[...])
    gain = dot(first_hi, incidence_t[...]) + dot(first_lo, incidence_t[...])
    gain_hi[...], gain_lo[...] = split(gain)
    series_hi[...] = jnp.zeros((DATE_LANES, PIXELS), BF16)
    series_lo[...] = jnp.zeros((DATE_LANES, PIXELS), BF16)

    for copy in gram_copies:
        copy.wait()
    solve_rows = []
    for tile, total in enumerate(gathered(gram_own, gram_got)):
        sums = jnp.sum(total, axis=1, keepdims=True)
        centre = ((block + tile - 1).astype(F32) * COLS + COLS // 2) / SLAB_COLS - 0.5
        g00, g01, g02 = sums[0:1] + 1.0, sums[1:2], sums[2:3] - centre
        g11, g12, g22 = sums[3:4] + 1.0, sums[4:5], sums[5:6] + (1.0 + centre * centre)
        c00, c01, c02 = g11 * g22 - g12 * g12, g02 * g12 - g01 * g22, g01 * g12 - g02 * g11
        c11, c12, c22 = g00 * g22 - g02 * g02, g01 * g02 - g00 * g12, g00 * g11 - g01 * g01
        determinant = g00 * c00 + g01 * c01 + g02 * c02
        _, along_u, along_v = basis_rows[tile]
        member = lanes([members[tile][0:1], members[tile][1:2]])
        for first, second, third in ((c00, c01, c02), (c01, c11, c12), (c02, c12, c22)):
            solve_rows.append(
                member * ((first + second * along_u + third * along_v) / determinant)
            )
        solve_rows.append(jnp.zeros((1, PIXELS), F32))
    solve_rows.append(jnp.zeros((4, PIXELS), F32))
    solve_v[...] = jnp.concatenate(solve_rows, axis=0)
    solve_store = pltpu.make_async_copy(solve_v, solve_out, store_sem.at[0])
    solve_store.start()
    weight_rows = []
    for tile in range(3):
        weight = lanes([weights[tile][0:1], weights[tile][1:2]])
        weight_rows += [weight * row for row in basis_rows[tile]]
        weight_rows.append(jnp.zeros((1, PIXELS), F32))
    weight_rows.append(jnp.zeros((4, PIXELS), F32))
    moment_weights = jnp.concatenate(weight_rows, axis=0).astype(BF16)
    coh_lanes = lanes([coh[0:1], coh[1:2]])

    small[4].wait()
    pltpu.make_async_copy(
        stacked.at[pl.ds(0, IFGS - OWN_IFGS)], stacked.at[pl.ds(0, IFGS - OWN_IFGS)], phase_recv
    ).wait()

    wide[...] = stacked.reshape(ROWS * IFGS, COLS)[...].astype(F32)
    for row in range(ROWS):
        values[:, COLS * row : COLS * row + COLS] = wide[pl.ds(row, IFGS, stride=ROWS), :]
    values_half[...] = values[...].astype(BF16)
    series[...] = dot(gain_hi[...], values_half[...]) + dot(gain_lo[...], values_half[...])
    for sweep in range(REWEIGHTS):
        series_hi[0:DATE_ROWS, :], series_lo[0:DATE_ROWS, :] = split(series[...])
        residual = values[...] - (
            dot(incidence[...], series_hi[...]) + dot(incidence[...], series_lo[...])
        )
        square = residual * residual
        scale = jnp.sum(square, axis=0, keepdims=True) * (1.0 / IFGS) + 1e-6
        ratio = scale / (square + scale)
        pull_hi[...], pull_lo[...] = split(coh_lanes * (ratio * ratio) * residual)
        series[...] = series[...] + (
            dot(gain_hi[...], pull_hi[...])
            + dot(gain_hi[...], pull_lo[...])
            + dot(gain_lo[...], pull_hi[...])
        )
    series_hi[0:DATE_ROWS, :], series_lo[0:DATE_ROWS, :] = split(series[...])
    series_store = pltpu.make_async_copy(series, series_out, store_sem.at[1])
    series_store.start()

    over_pixels = (((1,), (1,)), ((), ()))
    moments = lax.dot_general(
        moment_weights, series_hi[...], over_pixels, preferred_element_type=F32
    ) + lax.dot_general(moment_weights, series_lo[...], over_pixels, preferred_element_type=F32)
    for tile in range(3):
        moments_own[tile] = moments[4 * tile : 4 * tile + 4, :]
    moment_copies = trade(moments_own, moments_got, moment_send, moment_recv)
    for copy in moment_copies:
        copy.wait()
    moments_all[...] = jnp.concatenate(
        gathered(moments_own, moments_got) + [jnp.zeros((4, DATE_LANES), F32)], axis=0
    )
    moments_store = pltpu.make_async_copy(moments_all, moments_out, store_sem.at[2])
    moments_store.start()

    pltpu.make_async_copy(
        phases.at[:, :, pl.ds(COLS, (STACK - 1) * COLS)],
        phases.at[:, :, pl.ds(COLS, (STACK - 1) * COLS)],
        phase_send,
    ).wait()
    solve_store.wait()
    series_store.wait()
    moments_store.wait()


def deramp_kernel(series, moments, solve, out):
    over_terms = (((0,), (0,)), ((), ()))
    m_hi, m_lo = split(moments[...])
    s_hi, s_lo = split(solve[...])
    plane = lax.dot_general(
        jnp.concatenate([m_hi, m_lo, m_hi], axis=0),
        jnp.concatenate([s_hi, s_hi, s_lo], axis=0),
        over_terms,
        preferred_element_type=F32,
    )
    flat = series[0:DATES, :] - plane[0:DATES, :]
    out_rows = out.reshape(DATES * ROWS, COLS)
    for row in range(ROWS):
        out_rows[pl.ds(row, DATES, stride=ROWS), :] = flat[:, COLS * row : COLS * row + COLS]


def local(phases, ifg_pairs, preconditioner, coherence, geo_tiles):
    anywhere = pl.BlockSpec(memory_space=pl.ANY)
    vmem = pl.BlockSpec(memory_space=pltpu.VMEM)
    dma = pltpu.SemaphoreType.DMA
    series, moments, solve = pl.pallas_call(
        invert_kernel,
        out_shape=(
            jax.ShapeDtypeStruct((DATE_ROWS, PIXELS), F32),
            jax.ShapeDtypeStruct((16, DATE_LANES), F32),
            jax.ShapeDtypeStruct((16, PIXELS), F32),
        ),
        in_specs=[anywhere] * 5,
        out_specs=(anywhere,) * 3,
        scratch_shapes=[
            pltpu.VMEM((IFGS, ROWS, COLS), BF16),
            pltpu.VMEM((ROWS * IFGS, COLS), F32),
            pltpu.VMEM((IFGS, PIXELS), F32),
            pltpu.VMEM((IFGS, PIXELS), BF16),
            pltpu.VMEM((2, IFGS), jnp.int32),
            pltpu.VMEM((DATES, DATES), F32),
            pltpu.VMEM((DATE_ROWS, DATE_LANES), F32),
            pltpu.VMEM((ROWS, COLS), jnp.int32),
            pltpu.VMEM((ROWS, COLS), jnp.int32),
            pltpu.VMEM((IFGS, DATE_LANES), BF16),
            pltpu.VMEM((DATE_LANES, IFGS), BF16),
            pltpu.VMEM((DATE_ROWS, IFGS), BF16),
            pltpu.VMEM((DATE_ROWS, IFGS), BF16),
            pltpu.VMEM((DATE_ROWS, PIXELS), F32),
            pltpu.VMEM((DATE_LANES, PIXELS), BF16),
            pltpu.VMEM((DATE_LANES, PIXELS), BF16),
            pltpu.VMEM((IFGS, PIXELS), BF16),
            pltpu.VMEM((IFGS, PIXELS), BF16),
            pltpu.VMEM((3, 8, COLS), F32),
            pltpu.VMEM((2, 5, 3, 8, COLS), F32),
            pltpu.VMEM((3, 4, DATE_LANES), F32),
            pltpu.VMEM((2, 5, 3, 4, DATE_LANES), F32),
            pltpu.VMEM((16, DATE_LANES), F32),
            pltpu.VMEM((16, PIXELS), F32),
            dma((5,)),
            dma((3,)),
            dma,
            dma,
            dma((2, 5)),
            dma((2, 5)),
            dma((2, 5)),
            dma((2, 5)),
        ],
        compiler_params=pltpu.CompilerParams(
            collective_id=0, has_side_effects=True, vmem_limit_bytes=56 * 2**20
        ),
    )(phases, ifg_pairs.T, preconditioner, coherence, geo_tiles)
    return pl.pallas_call(
        deramp_kernel,
        out_shape=jax.ShapeDtypeStruct((DATES, ROWS, COLS), F32),
        in_specs=[vmem] * 3,
        out_specs=vmem,
    )(series, moments, solve)


def solution(mesh):
    return jax.shard_map(
        local,
        mesh=mesh,
        in_specs=(
            P("stack", "azimuth", "range"),
            P(),
            P(),
            P("azimuth", ("range", "stack")),
            P("azimuth", ("range", "stack")),
        ),
        out_specs=P(None, "azimuth", ("range", "stack")),
        check_vma=False,
    )
```

time: 212 us -> 54.7 us (0.26)
  the two profiles are of different devices: /device:TPU:4 before, /device:TPU:1 now
where the time goes in v1:
time: 54.7 us; the launch traced here: 54.6 us
  Pallas kernels  54.6 us (100%)
    pallas_call x1, Pallas kernels, local(): pl.pallas_call(invert_kernel, out_shape=(jax.ShapeDtypeStruct((DATE_ROWS,...  52.4 us
    pallas_call x1, Pallas kernels, local(): pl.pallas_call(deramp_kernel, out_shape=jax.ShapeDtypeStruct((DATES, ROWS...  2.2 us

profile of v1, /device:TPU:1, one launch (start us, length us, event | category | flops | bytes accessed | tf_op | source)
XLA Modules:
  0.0 54.6 jit_solution(5314481389828469371)
XLA Ops:
  0.0 52.4 %shard_map.55 = (f32[608,256]{1,0:T(8,128)}, f32[16,640]{1,0:T(8,128)}, f32[16,256]{1,0:T(8,128)}) custom-call(bf16[9,2,16384]{2,1,0:T(2,128)(2,1)} %phases.1, s32[2,1152]{1,0:T(2,128)} %bitcast.1, f32[600,600]{1,0:T(8,128)} %precond.1, s32[2,128]{1,0:T(2,128)} %coherence.1, s32[2,128]{1,0:T(2,128)} %tiles.1), custom_call_target="tpu_custom_call" | custom-call | tf_op jit(solution)/shard_map/pallas_call | solution.py:347
  52.4 2.2 %shard_map.56 = f32[600,2,128]{2,1,0:T(2,128)} custom-call(f32[608,256]{1,0:T(8,128)} %get-tuple-element.8.series, f32[16,640]{1,0:T(8,128)} %get-tuple-element.9.moments, f32[16,256]{1,0:T(8,128)} %get-tuple-element.10.solve), custom_call_target="tpu_custom_call" | custom-call | tf_op jit(solution)/shard_map/pallas_call | solution.py:394

commit v2 on v1

--- a/solution.py
+++ b/solution.py
@@ -25,6 +25,7 @@
 OWN_IFGS = IFGS // STACK
 BLOCKS = SLAB_COLS // COLS
 REACH = (-2, -1, 0, 1, 2)
+IFG_PARTS = (slice(0, 512), slice(512, 1152))
 
 
 def split(value):
@@ -69,8 +70,8 @@
     gain_hi,
     gain_lo,
     series,
-    series_hi,
-    series_lo,
+    halves,
+    residual,
     pull_hi,
     pull_lo,
     gram_own,
@@ -105,13 +106,15 @@
 
     barrier = pltpu.get_barrier_semaphore()
 
-    def greet(step, carry):
+    def neighbour(dz, dy, dc):
+        return (
+            lax.rem(z + dz, SIDE) * (2 * SIDE) + lax.rem(y + dy, SIDE) * 2 + lax.rem(core + dc, 2)
+        )
+
+    for step in far_first():
         pl.semaphore_signal(
-            barrier, inc=1, device_id={"stack": lax.rem(me + step, STACK)}, device_id_type=MESH
+            barrier, inc=1, device_id={"stack": neighbour(*step)}, device_id_type=MESH
         )
-        return carry
-
-    lax.fori_loop(1, STACK, greet, 0)
     for reach, other in group:
         pl.semaphore_signal(barrier, inc=1, device_id=peer(reach, other), device_id_type=MESH)
 
@@ -131,10 +134,8 @@
 
     pl.semaphore_wait(barrier, STACK - 1 + len(group))
 
-    for dz, dy, dc in far_first():
-        there = (
-            lax.rem(z + dz, SIDE) * (2 * SIDE) + lax.rem(y + dy, SIDE) * 2 + lax.rem(core + dc, 2)
-        )
+    for step in far_first():
+        there = neighbour(*step)
         pltpu.make_async_remote_copy(
             src_ref=phases.at[:, :, pl.ds(pl.multiple_of(there * COLS, COLS), COLS)],
             dst_ref=stacked.at[pl.ds(OWN_IFGS * me, OWN_IFGS)],
@@ -185,14 +186,16 @@
             axis=0,
         )
 
-    def trade(own, got, send_sem, recv_sem):
+    def trade(own, got, unit, send_sem, recv_sem):
         copies = []
         for reach, other in group:
             first, last = max(0, reach), min(3, 3 + reach)
             copies.append(
                 pltpu.make_async_remote_copy(
-                    src_ref=own.at[pl.ds(first, last - first)],
-                    dst_ref=got.at[other, reach + 2, pl.ds(first - reach, last - first)],
+                    src_ref=own.at[pl.ds(unit * first, unit * (last - first))],
+                    dst_ref=got.at[
+                        other, reach + 2, pl.ds(unit * (first - reach), unit * (last - first))
+                    ],
                     send_sem=send_sem.at[other, reach + 2],
                     recv_sem=recv_sem.at[other, reach + 2],
                     device_id=peer(reach, other),
@@ -203,17 +206,17 @@
             copy.start()
         return copies
 
-    def gathered(own, got):
+    def gathered(own, got, unit):
         totals = []
-        for tile in range(3):
-            total = own[tile]
+        for place in range(3 * unit):
+            total = own[place]
             for reach, other in group:
-                if max(0, reach) - reach <= tile < min(3, 3 + reach) - reach:
-                    total = total + got[other, reach + 2, tile]
+                if max(0, reach) - reach <= place // unit < min(3, 3 + reach) - reach:
+                    total = total + got[other, reach + 2, place]
             totals.append(total)
         return totals
 
-    gram_copies = trade(gram_own, gram_got, gram_send, gram_recv)
+    gram_copies = trade(gram_own, gram_got, 1, gram_send, gram_recv)
 
     small[2].wait()
     earlier, later = pairs_v[0:1, :], pairs_v[1:2, :]
@@ -227,23 +230,24 @@
         date_lanes = (
             lax.broadcasted_iota(jnp.int32, (IFGS, 128), 1) + 128 * part
         ).astype(F32)
-        incidence[:, 128 * part : 128 * part + 128] = (
+        columns = (
             jnp.where(later_col == date_lanes, 1.0, 0.0)
             - jnp.where(earlier_col == date_lanes, 1.0, 0.0)
         ).astype(BF16)
+        incidence[:, 128 * part : 128 * part + 128] = columns
+        incidence[:, DATE_LANES + 128 * part : DATE_LANES + 128 * part + 128] = columns
     precond_pad[...] = jnp.zeros((DATE_ROWS, DATE_LANES), F32)
     small[3].wait()
     precond_pad[0:DATES, 0:DATES] = precond_v[...]
     first_hi, first_lo = split(precond_pad[...])
     gain = dot(first_hi, incidence_t[...]) + dot(first_lo, incidence_t[...])
     gain_hi[...], gain_lo[...] = split(gain)
-    series_hi[...] = jnp.zeros((DATE_LANES, PIXELS), BF16)
-    series_lo[...] = jnp.zeros((DATE_LANES, PIXELS), BF16)
+    halves[...] = jnp.zeros((2 * DATE_LANES, PIXELS), BF16)
 
     for copy in gram_copies:
         copy.wait()
     solve_rows = []
-    for tile, total in enumerate(gathered(gram_own, gram_got)):
+    for tile, total in enumerate(gathered(gram_own, gram_got, 1)):
         sums = jnp.sum(total, axis=1, keepdims=True)
         centre = ((block + tile - 1).astype(F32) * COLS + COLS // 2) / SLAB_COLS - 0.5
         g00, g01, g02 = sums[0:1] + 1.0, sums[1:2], sums[2:3] - centre
@@ -257,8 +261,7 @@
             solve_rows.append(
                 member * ((first + second * along_u + third * along_v) / determinant)
             )
-        solve_rows.append(jnp.zeros((1, PIXELS), F32))
-    solve_rows.append(jnp.zeros((4, PIXELS), F32))
+    solve_rows.append(jnp.zeros((7, PIXELS), F32))
     solve_v[...] = jnp.concatenate(solve_rows, axis=0)
     solve_store = pltpu.make_async_copy(solve_v, solve_out, store_sem.at[0])
     solve_store.start()
@@ -276,40 +279,62 @@
         stacked.at[pl.ds(0, IFGS - OWN_IFGS)], stacked.at[pl.ds(0, IFGS - OWN_IFGS)], phase_recv
     ).wait()
 
-    wide[...] = stacked.reshape(ROWS * IFGS, COLS)[...].astype(F32)
-    for row in range(ROWS):
-        values[:, COLS * row : COLS * row + COLS] = wide[pl.ds(row, IFGS, stride=ROWS), :]
-    values_half[...] = values[...].astype(BF16)
-    series[...] = dot(gain_hi[...], values_half[...]) + dot(gain_lo[...], values_half[...])
+    flat = stacked.reshape(ROWS * IFGS, COLS)
+    total = jnp.zeros((DATE_ROWS, PIXELS), F32)
+    for part in IFG_PARTS:
+        first = ROWS * part.start
+        wide[first : ROWS * part.stop, :] = flat[first : ROWS * part.stop, :].astype(F32)
+        for row in range(ROWS):
+            lane = slice(COLS * row, COLS * row + COLS)
+            column = wide[pl.ds(first + row, part.stop - part.start, stride=ROWS), :]
+            values[part, lane] = column
+            values_half[part, lane] = column.astype(BF16)
+        total = total + dot(gain_hi[:, part], values_half[part, :])
+        total = total + dot(gain_lo[:, part], values_half[part, :])
+    series[...] = total
+
+    def halve():
+        high, low = split(series[...])
+        halves[0:DATE_ROWS, :] = high
+        halves[DATE_LANES : DATE_LANES + DATE_ROWS, :] = low
+
     for sweep in range(REWEIGHTS):
-        series_hi[0:DATE_ROWS, :], series_lo[0:DATE_ROWS, :] = split(series[...])
-        residual = values[...] - (
-            dot(incidence[...], series_hi[...]) + dot(incidence[...], series_lo[...])
-        )
-        square = residual * residual
-        scale = jnp.sum(square, axis=0, keepdims=True) * (1.0 / IFGS) + 1e-6
-        ratio = scale / (square + scale)
-        pull_hi[...], pull_lo[...] = split(coh_lanes * (ratio * ratio) * residual)
-        series[...] = series[...] + (
-            dot(gain_hi[...], pull_hi[...])
-            + dot(gain_hi[...], pull_lo[...])
-            + dot(gain_lo[...], pull_hi[...])
-        )
-    series_hi[0:DATE_ROWS, :], series_lo[0:DATE_ROWS, :] = split(series[...])
+        halve()
+        squares = jnp.zeros((8, PIXELS), F32)
+        for part in range(2):
+            rows = slice(IFGS // 2 * part, IFGS // 2 * (part + 1))
+            misfit = values[rows, :] - dot(incidence[rows, :], halves[...])
+            residual[rows, :] = misfit
+            squares = squares + jnp.sum((misfit * misfit).reshape(IFGS // 16, 8, PIXELS), axis=0)
+        scale = jnp.sum(squares, axis=0, keepdims=True) * (1.0 / IFGS) + 1e-6
+        coherent_scale = coh_lanes * scale
+        total = series[...]
+        for part in IFG_PARTS:
+            misfit = residual[part, :]
+            ratio = coherent_scale / (misfit * misfit + scale)
+            pull_hi[part, :], pull_lo[part, :] = split((ratio * ratio) * misfit)
+            total = total + dot(gain_hi[:, part], pull_hi[part, :])
+            total = total + dot(gain_lo[:, part], pull_hi[part, :])
+            total = total + dot(gain_hi[:, part], pull_lo[part, :])
+        series[...] = total
+    halve()
     series_store = pltpu.make_async_copy(series, series_out, store_sem.at[1])
     series_store.start()
 
     over_pixels = (((1,), (1,)), ((), ()))
     moments = lax.dot_general(
-        moment_weights, series_hi[...], over_pixels, preferred_element_type=F32
-    ) + lax.dot_general(moment_weights, series_lo[...], over_pixels, preferred_element_type=F32)
+        moment_weights, halves[0:DATE_LANES, :], over_pixels, preferred_element_type=F32
+    ) + lax.dot_general(
+        moment_weights, halves[DATE_LANES:, :], over_pixels, preferred_element_type=F32
+    )
     for tile in range(3):
-        moments_own[tile] = moments[4 * tile : 4 * tile + 4, :]
-    moment_copies = trade(moments_own, moments_got, moment_send, moment_recv)
+        for term in range(3):
+            moments_own[3 * tile + term] = moments[4 * tile + term : 4 * tile + term + 1, :]
+    moment_copies = trade(moments_own, moments_got, 3, moment_send, moment_recv)
     for copy in moment_copies:
         copy.wait()
     moments_all[...] = jnp.concatenate(
-        gathered(moments_own, moments_got) + [jnp.zeros((4, DATE_LANES), F32)], axis=0
+        gathered(moments_own, moments_got, 3) + [jnp.zeros((7, DATE_LANES), F32)], axis=0
     )
     moments_store = pltpu.make_async_copy(moments_all, moments_out, store_sem.at[2])
     moments_store.start()
@@ -324,7 +349,17 @@
     moments_store.wait()
 
 
-def deramp_kernel(series, moments, solve, out):
+def deramp_kernel(series_in, moments_in, solve_in, out, series, moments, solve, load_sem):
+    copies = [
+        pltpu.make_async_copy(source, target, load_sem.at[place])
+        for place, (source, target) in enumerate(
+            ((moments_in, moments), (solve_in, solve), (series_in, series))
+        )
+    ]
+    for copy in copies:
+        copy.start()
+    for copy in copies:
+        copy.wait()
     over_terms = (((0,), (0,)), ((), ()))
     m_hi, m_lo = split(moments[...])
     s_hi, s_lo = split(solve[...])
@@ -342,6 +377,7 @@
 
 def local(phases, ifg_pairs, preconditioner, coherence, geo_tiles):
     anywhere = pl.BlockSpec(memory_space=pl.ANY)
+    hbm = pl.BlockSpec(memory_space=pltpu.HBM)
     vmem = pl.BlockSpec(memory_space=pltpu.VMEM)
     dma = pltpu.SemaphoreType.DMA
     series, moments, solve = pl.pallas_call(
@@ -351,7 +387,7 @@
             jax.ShapeDtypeStruct((16, DATE_LANES), F32),
             jax.ShapeDtypeStruct((16, PIXELS), F32),
         ),
-        in_specs=[anywhere] * 5,
+        in_specs=[hbm] * 5,
         out_specs=(anywhere,) * 3,
         scratch_shapes=[
             pltpu.VMEM((IFGS, ROWS, COLS), BF16),
@@ -363,19 +399,19 @@
             pltpu.VMEM((DATE_ROWS, DATE_LANES), F32),
             pltpu.VMEM((ROWS, COLS), jnp.int32),
             pltpu.VMEM((ROWS, COLS), jnp.int32),
-            pltpu.VMEM((IFGS, DATE_LANES), BF16),
+            pltpu.VMEM((IFGS, 2 * DATE_LANES), BF16),
             pltpu.VMEM((DATE_LANES, IFGS), BF16),
             pltpu.VMEM((DATE_ROWS, IFGS), BF16),
             pltpu.VMEM((DATE_ROWS, IFGS), BF16),
             pltpu.VMEM((DATE_ROWS, PIXELS), F32),
-            pltpu.VMEM((DATE_LANES, PIXELS), BF16),
-            pltpu.VMEM((DATE_LANES, PIXELS), BF16),
+            pltpu.VMEM((2 * DATE_LANES, PIXELS), BF16),
+            pltpu.VMEM((IFGS, PIXELS), F32),
             pltpu.VMEM((IFGS, PIXELS), BF16),
             pltpu.VMEM((IFGS, PIXELS), BF16),
             pltpu.VMEM((3, 8, COLS), F32),
             pltpu.VMEM((2, 5, 3, 8, COLS), F32),
-            pltpu.VMEM((3, 4, DATE_LANES), F32),
-            pltpu.VMEM((2, 5, 3, 4, DATE_LANES), F32),
+            pltpu.VMEM((9, 1, DATE_LANES), F32),
+            pltpu.VMEM((2, 5, 9, 1, DATE_LANES), F32),
             pltpu.VMEM((16, DATE_LANES), F32),
             pltpu.VMEM((16, PIXELS), F32),
             dma((5,)),
@@ -388,14 +424,24 @@
             dma((2, 5)),
         ],
         compiler_params=pltpu.CompilerParams(
-            collective_id=0, has_side_effects=True, vmem_limit_bytes=56 * 2**20
+            collective_id=0, has_side_effects=True, vmem_limit_bytes=40 * 2**20
         ),
-    )(phases, ifg_pairs.T, preconditioner, coherence, geo_tiles)
+    )(*(
+        pltpu.with_memory_space_constraint(array, pltpu.HBM)
+        for array in (phases, ifg_pairs.T, preconditioner, coherence, geo_tiles)
+    ))
     return pl.pallas_call(
         deramp_kernel,
         out_shape=jax.ShapeDtypeStruct((DATES, ROWS, COLS), F32),
-        in_specs=[vmem] * 3,
+        in_specs=[anywhere] * 3,
         out_specs=vmem,
+        scratch_shapes=[
+            pltpu.VMEM((DATE_ROWS, PIXELS), F32),
+            pltpu.VMEM((16, DATE_LANES), F32),
+            pltpu.VMEM((16, PIXELS), F32),
+            dma((3,)),
+        ],
+        compiler_params=pltpu.CompilerParams(vmem_limit_bytes=16 * 2**20),
     )(series, moments, solve)
 
 

time: 54.7 us -> 53.2 us (0.973)
  Pallas kernels: 54.6 us -> 52.9 us
    pallas_call x1, Pallas kernels: 2.2 us -> 1.36 us  [local(): pl.pallas_call(deramp_kernel, out_shape=jax.ShapeDtypeStruct((DATES, ROWS...]
    pallas_call x1, Pallas kernels: 52.4 us -> 51.6 us  [local(): pl.pallas_call(invert_kernel, out_shape=(jax.ShapeDtypeStruct((DATE_ROWS,...]
where the time goes in v2:
time: 53.2 us; the launch traced here: 53.1 us
  Pallas kernels  52.9 us (99%)
    pallas_call x1, Pallas kernels, local(): pl.pallas_call(invert_kernel, out_shape=(jax.ShapeDtypeStruct((DATE_ROWS,...  51.6 us
    pallas_call x1, Pallas kernels, local(): pl.pallas_call(deramp_kernel, out_shape=jax.ShapeDtypeStruct((DATES, ROWS...  1.36 us

profile of v2, /device:TPU:1, one launch (start us, length us, event | category | flops | bytes accessed | tf_op | source)
XLA Modules:
  0.0 53.1 jit_solution(17477202150350642329)
XLA Ops:
  0.0 51.6 %shard_map.55 = (f32[608,256]{1,0:T(8,128)S(1)}, f32[16,640]{1,0:T(8,128)S(1)}, f32[16,256]{1,0:T(8,128)S(1)}) custom-call(bf16[9,2,16384]{2,1,0:T(2,128)(2,1)} %phases.1, s32[2,1152]{1,0:T(2,128)} %bitcast.1, f32[600,600]{1,0:T(8,128)} %precond.1, s32[2,128]{1,0:T(2,128)} %coherence.1, s32[2,128]{1,0:T(2,128)} %tiles.1), custom_call_target="tpu_custom_call" | custom-call | tf_op jit(solution)/shard_map/pallas_call | solution.py:383
  51.6 1.4 %shard_map.56 = f32[600,2,128]{2,1,0:T(2,128)} custom-call(f32[608,256]{1,0:T(8,128)S(1)} %get-tuple-element.8.series_in, f32[16,640]{1,0:T(8,128)S(1)} %get-tuple-element.9.moments_in, f32[16,256]{1,0:T(8,128)S(1)} %get-tuple-element.10.solve_in), custom_call_target="tpu_custom_call" | custom-call | tf_op jit(solution)/shard_map/pallas_call | solution.py:433
